TPU v7x, 256 devices: a whole 4x4x8 slice. The times are simulated.
256 devices in a mesh: expert: 128 (over x, z, y), dp: 2 (over core).
Axes of the slice: x: 4, y: 4, z: 8, core: 2. Of those that a mesh axis runs over, the one named last changes fastest.
Arguments:
- tokens: bfloat16 [16384, 4096], P(('expert', 'dp')), may hold values from -6 to 6
- routes: int32 [16384, 8], P(('expert', 'dp')), may hold values from 0 to 127, all different within a row; in each aligned block of 64 rows (0 to 63, 64 to 127, ...) at most 8 rows name the same one
- gate_probs: float32 [16384, 8], P(('expert', 'dp')), may hold values from 0.05 to 0.35
- gate_w: bfloat16 [128, 4096, 768], P('expert', None, 'dp'), may hold values from -0.09375 to 0.09375
- up_w: bfloat16 [128, 4096, 768], P('expert', None, 'dp'), may hold values from -0.09375 to 0.09375
- down_w: bfloat16 [128, 768, 4096], P('expert', 'dp'), may hold values from -0.21875 to 0.21875
Outputs:
- mixed_out: bfloat16 [16384, 4096], P(('expert', 'dp'))
Inputs may be any that keep to these rules, and one draw needn't show every extreme that they name: `routes`: each token names 8 different experts. Among the 64 tokens of one device (aligned blocks of rows), no expert is named by more than 8 tokens; in some block an expert is named by exactly 8 tokens.
All inputs are finite; a program needn't handle non-finite values.
Results may differ from a plain program's by a relative error of at most 0.0057.
Values may be sent and summed in bfloat16 or wider, within the bound.
No kernel may reach another device: no remote copies, remote signals or barrier semaphores. Data moves between devices by JAX's collectives and lax.ppermute only.
A program may use at most 192 MiB of HBM per device.

v0:
```python
import jax
import jax.numpy as jnp
from jax import lax
from jax.sharding import PartitionSpec as P


def swiglu(row_block, w_gate, w_up, w_down):
    gate_act = jnp.dot(row_block, w_gate, preferred_element_type=jnp.float32)
    up_act = jnp.dot(row_block, w_up, preferred_element_type=jnp.float32)
    hidden = (jax.nn.silu(gate_act) * up_act).astype(jnp.bfloat16)
    return jnp.dot(hidden, w_down, preferred_element_type=jnp.float32)


def apply_expert(row_block, w_gate, w_up, w_down):
    return swiglu(row_block, w_gate, w_up, w_down)


def body(tokens, routes, gate_probs, gate_w, up_w, down_w):
    experts = lax.axis_size("expert")
    tok_count, model_width = tokens.shape
    top_count = routes.shape[1]
    capacity = 2 * tok_count * top_count // experts
    expert_ids = jnp.arange(experts, dtype=jnp.int32)
    named_hits = jnp.sum((routes[:, :, None] == expert_ids).astype(jnp.int32), axis=1)
    before = jnp.cumsum(named_hits, axis=0) - named_hits
    slot_index = jnp.take_along_axis(before, routes, axis=1)
    target = routes * capacity + slot_index
    buffer_rows = jnp.arange(experts * capacity, dtype=jnp.int32)
    placer = jnp.sum(
        (target[None, :, :] == buffer_rows[:, None, None]).astype(jnp.float32), axis=2
    ).astype(jnp.bfloat16)
    outgoing = jnp.dot(placer, tokens, preferred_element_type=jnp.float32).astype(jnp.bfloat16)
    outgoing = outgoing.reshape(experts, capacity, model_width)
    present = (
        jnp.sum(placer.astype(jnp.float32), axis=1).astype(jnp.bfloat16).reshape(experts, capacity)
    )
    w_gate = gate_w[0]
    w_up = up_w[0]
    w_down = down_w[0]
    row_block = lax.all_to_all(outgoing, "expert", split_axis=0, concat_axis=0, tiled=True)
    flag_block = lax.all_to_all(present, "expert", split_axis=0, concat_axis=0, tiled=True)
    source_count = row_block.shape[0]
    item_count = row_block.shape[1]
    flat_rows = row_block.reshape(-1, model_width)
    flat_flags = flag_block.reshape(-1)
    both_rows = lax.all_gather(flat_rows, "dp", axis=0, tiled=True)
    partial_out = apply_expert(both_rows, w_gate, w_up, w_down)
    result = lax.psum_scatter(partial_out, "dp", scatter_dimension=0, tiled=True)
    masked = result * flat_flags.astype(jnp.float32)[:, None]
    answered = masked.astype(jnp.bfloat16).reshape(source_count, item_count, model_width)
    returned = lax.all_to_all(answered, "expert", split_axis=0, concat_axis=0, tiled=True)
    picked = returned.reshape(experts * capacity, model_width)[target]
    mixed_out = jnp.einsum(
        "tk,tkd->td", gate_probs, picked.astype(jnp.float32), precision=lax.Precision.HIGHEST
    )
    return mixed_out.astype(jnp.bfloat16)


def solution(mesh):
    return jax.shard_map(
        body,
        mesh=mesh,
        in_specs=(
            P(("expert", "dp"), None),
            P(("expert", "dp"), None),
            P(("expert", "dp"), None),
            P("expert", None, "dp"),
            P("expert", None, "dp"),
            P("expert", "dp", None),
        ),
        out_specs=P(("expert", "dp"), None),
        check_vma=False,
    )
```

profile of v0, /device:TPU:2, one launch (start us, length us, event | category | flops | bytes accessed | tf_op | source)
XLA Modules:
  0.0 579.9 jit_solution(941686837038767233)
XLA Ops:
  6.5 0.0 copy-start
  6.5 0.0 all-gather.2.cloned.1.call-start
  6.5 0.8 bitcast_or_fusion
  7.4 0.9 copy.35
  8.3 0.1 copy.36
  8.4 0.1 reshape.50
  8.4 0.1 convert_reduce_fusion.1
  8.6 0.1 reduce_window_sum.11
  8.7 0.0 copy-start.2
  8.7 3.6 gather_fusion.1
  12.3 0.1 reshape.53
  12.4 0.1 copy.37
  12.5 0.0 copy-done.2
  12.5 0.1 copy.38
  12.6 0.7 convert_reduce_fusion
  13.3 3.4 convert_bitcast_fusion
  16.7 201.5 %all_to_all.20 = bf16[128,8,4096]{2,1,0:T(8,128)(2,1)} all-to-all(bf16[128,8,4096]{2,1,0:T(8,128)(2,1)S(1)} %convert_bitcast_fusion), channel_id=1, replica_groups=mesh['expert'=128,'dp'=2] {'expert'}, dimensions={0} | all-to-all | bytes 16777216 | tf_op jit(solution)/shard_map/all_to_all | solution.py:40
  218.2 0.0 all-gather.2.cloned.1.call-update
  218.3 0.2 reduce-scatter.2.cloned.1.call-start
  218.5 31.1 %all-gather.2.cloned.1.call-done = bf16[2048,4096]{1,0:T(8,128)(2,1)} async-done(((bf16[1024,4096]{1,0:T(8,128)(2,1)}), bf16[2048,4096]{1,0:T(8,128)(2,1)}) %all-gather.2.cloned.1.call-update) | async-done | bytes 16777232 | tf_op jit(solution)/shard_map/all_gather | solution.py:46
  249.6 0.0 copy-start.4
  249.6 13.0 %fusion.6 = f32[2048,384]{1,0:T(8,128)S(1)} fusion(bf16[2048,4096]{1,0:T(8,128)(2,1)} %all-gather.2.cloned.1.call-done, bf16[1,4096,384]{2,1,0:T(8,128)(2,1)} %param.9), kind=kOutput, calls=%fused_computation.11 | convolution fusion | flops 6442450944 | bytes 23068672 | tf_op jit(solution)/shard_map/dot_general | solution.py:8
  262.6 0.0 copy-done.4
  262.6 12.5 %fusion.8 = bf16[2048,384]{1,0:T(8,128)(2,1)S(1)} fusion(bf16[2048,4096]{1,0:T(8,128)(2,1)} %all-gather.2.cloned.1.call-done, bf16[1,4096,384]{2,1,0:T(8,128)(2,1)S(1)} %copy-done.4, f32[2048,384]{1,0:T(8,128)S(1)} %fusion.6), kind=kOutput, calls=%fused_computation.13 | convolution fusion | flops 6447169536 | bytes 24641536 | tf_op jit(solution)/shard_map/dot_general | solution.py:9
  275.2 0.0 copy-done
  275.2 14.5 %fusion.3 = f32[2048,4096]{1,0:T(8,128)} fusion(bf16[2048,384]{1,0:T(8,128)(2,1)S(1)} %fusion.8, bf16[1,384,4096]{2,1,0:T(8,128)(2,1)S(1)} %copy-done), kind=kOutput, calls=%fused_computation.8 | convolution fusion | flops 6442450944 | bytes 38273024 | tf_op jit(solution)/shard_map/dot_general | solution.py:11
  289.6 0.0 reduce-scatter.2.cloned.1.call-update
  289.7 0.1 all_to_all.16
  289.8 24.6 %all_to_all.21 = bf16[128,1,8]{2,1,0:T(2,128)(2,1)S(1)} all-to-all(bf16[128,1,8]{2,1,0:T(2,128)(2,1)S(1)} %all_to_all.16), channel_id=1, replica_groups=mesh['expert'=128,'dp'=2] {'expert'}, dimensions={0} | all-to-all | bytes 4096 | tf_op jit(solution)/shard_map/all_to_all | solution.py:41
  314.4 0.2 convert_reduce_fusion.2
  314.6 0.1 reshape.41
  314.7 27.0 %reduce-scatter.2.cloned.1.call-done = f32[1024,4096]{1,0:T(8,128)} async-done(((f32[2048,4096]{1,0:T(8,128)}), f32[1024,4096]{1,0:T(8,128)}) %reduce-scatter.2.cloned.1.call-update) | async-done | bytes 16777232 | tf_op jit(solution)/shard_map/reduce_scatter | solution.py:48
  341.6 9.3 %fusion = bf16[128,8,4096]{2,1,0:T(8,128)(2,1)} fusion(f32[1024,4096]{1,0:T(8,128)} %reduce-scatter.2.cloned.1.call-done, f32[1024]{0:T(1024)S(1)} %reshape.41), kind=kLoop, calls=%fused_computation.3 | loop fusion | flops 8388608 | bytes 25169920 | tf_op jit(solution)/shard_map/reshape | solution.py:50
  350.9 0.0 copy-start.3
  350.9 14.5 %all-to-all-start.2 = ((bf16[128,8,4096]{2,1,0:T(8,128)(2,1)}), bf16[128,8,4096]{2,1,0:T(8,128)(2,1)}, u32[]{:S(2)}, u32[]{:S(2)}) async-start(bf16[128,8,4096]{2,1,0:T(8,128)(2,1)} %fusion), calls=%async_computation.3 | async-start | bytes 16777216 | tf_op jit(solution)/shard_map/all_to_all | solution.py:51
  365.4 0.0 copy-done.3
  365.4 0.1 copy.41
  365.5 0.1 copy.40
  365.6 0.1 reshape.44
  365.7 187.1 %all-to-all-done.2 = bf16[128,8,4096]{2,1,0:T(8,128)(2,1)} async-done(((bf16[128,8,4096]{2,1,0:T(8,128)(2,1)}), bf16[128,8,4096]{2,1,0:T(8,128)(2,1)}, u32[]{:S(2)}, u32[]{:S(2)}) %all-to-all-start.2) | async-done | bytes 8388640 | tf_op jit(solution)/shard_map/all_to_all | solution.py:51
  552.8 0.0 copy-start.1
  552.8 13.2 %gather_fusion = bf16[512,4096]{1,0:T(8,128)(2,1)} fusion(bf16[1024,4096]{1,0:T(8,128)(2,1)} %bitcast.7, s32[1024]{0:T(1024)S(1)} %pad_clamp_fusion), kind=kCustom, calls=%fused_computation | custom fusion | bytes 8390656 | tf_op jit(solution)/shard_map/gather | solution.py:52
  565.9 5.7 fusion.1
  571.6 1.4 copy.44
  573.0 0.0 copy-done.1
  (4 shorter events, 0.1 us)
Async XLA Ops:
  6.5 268.6 %copy-start = (bf16[1,384,4096]{2,1,0:T(8,128)(2,1)S(1)}, bf16[1,384,4096]{2,1,0:T(8,128)(2,1)}, u32[]{:S(2)}) copy-start(bf16[1,384,4096]{2,1,0:T(8,128)(2,1)} %param.11) | copy-start | bytes 9437188
  6.5 243.1 %all-gather.2.cloned.1.call-start = ((), (), s32[]{:S(2)}) async-start(), calls=%async_computation.4 | async-start | bytes 25165824 | tf_op jit(solution)/shard_map/all_gather | solution.py:46
  8.7 3.8 copy-start.2
  218.3 123.3 %reduce-scatter.2.cloned.1.call-start = ((), (), s32[]{:S(2)}) async-start(), calls=%async_computation.5 | async-start | bytes 50331648 | tf_op jit(solution)/shard_map/reduce_scatter | solution.py:48
  249.6 13.0 %copy-start.4 = (bf16[1,4096,384]{2,1,0:T(8,128)(2,1)S(1)}, bf16[1,4096,384]{2,1,0:T(8,128)(2,1)}, u32[]{:S(2)}) copy-start(bf16[1,4096,384]{2,1,0:T(8,128)(2,1)} %param.10) | copy-start | bytes 9437188
  350.9 14.5 %copy-start.3 = (f32[64,8]{0,1:T(8,128)S(1)}, f32[64,8]{0,1:T(8,128)}, u32[]{:S(2)}) copy-start(f32[64,8]{0,1:T(8,128)} %param.8) | copy-start | bytes 6148
  350.9 201.8 %all-to-all-start.2 = ((bf16[128,8,4096]{2,1,0:T(8,128)(2,1)}), bf16[128,8,4096]{2,1,0:T(8,128)(2,1)}, u32[]{:S(2)}, u32[]{:S(2)}) async-start(bf16[128,8,4096]{2,1,0:T(8,128)(2,1)} %fusion), calls=%async_computation.3 | async-start | bytes 16777216 | tf_op jit(solution)/shard_map/all_to_all | solution.py:51
  552.8 20.3 %copy-start.1 = (bf16[1,384,4096]{2,1,0:T(8,128)(2,1)S(1)}, bf16[1,384,4096]{2,1,0:T(8,128)(2,1)}, u32[]{:S(2)}) copy-start(bf16[1,384,4096]{2,1,0:T(8,128)(2,1)} %param.11) | copy-start | bytes 9437188
Sparse Core Ops, SparseCore 0:
  218.4 31.1 all-gather.1
  289.8 51.7 reduce-scatter.1
where the time goes:
time: 580 us
  waiting for transfers between devices  245 us (42%)
  blocking collectives  226 us (39%)
  matrix products  49.1 us (8%)
  local copies, waits for them, and re-layouts  19.9 us (3%)
  starting transfers between devices  14.7 us (3%)
  between operations  13.5 us (2%)
  other arithmetic  11.3 us (2%)
    all_to_all x1, blocking collectives, body(): lax.all_to_all(outgoing, 'expert', split_axis=0, concat_axis=0, tiled=True)  202 us
    all_to_all x1, waiting for transfers between devices, body(): lax.all_to_all(answered, 'expert', split_axis=0, concat_axis=0, tiled=True)  187 us
    all_gather x1, waiting for transfers between devices, body(): both_rows = lax.all_gather(flat_rows, 'dp', axis=0, tiled=True)  31.1 us
    reduce_scatter x1, waiting for transfers between devices, body(): lax.psum_scatter(partial_out, 'dp', scatter_dimension=0, tiled=True)  27 us
    all_to_all x1, blocking collectives, body(): lax.all_to_all(present, 'expert', split_axis=0, concat_axis=0, tiled=True)  24.6 us
    dot_general x1, matrix products, swiglu(): return jnp.dot(hidden, w_down, preferred_element_type=jnp.float32)  14.5 us
    all_to_all x1, starting transfers between devices, body(): lax.all_to_all(answered, 'expert', split_axis=0, concat_axis=0, tiled=True)  14.5 us
    gather x1, local copies, waits for them, and re-layouts, body(): picked = returned.reshape(experts * capacity, model_width)[target]  13.2 us
  transfers between devices with their start and end apart: 3, of which 3 were waited for; matrix products, arithmetic and copies ran while one was open for 0% of the time, Pallas kernels for 0%

commit v1 on v0

--- a/solution.py
+++ b/solution.py
@@ -43,7 +43,9 @@
     item_count = row_block.shape[1]
     flat_rows = row_block.reshape(-1, model_width)
     flat_flags = flag_block.reshape(-1)
-    both_rows = lax.all_gather(flat_rows, "dp", axis=0, tiled=True)
+    both_rows = jnp.concatenate(
+        lax.all_to_all(jnp.stack([flat_rows] * lax.axis_size("dp")), "dp", 0, 0), axis=0
+    )
     partial_out = apply_expert(both_rows, w_gate, w_up, w_down)
     result = lax.psum_scatter(partial_out, "dp", scatter_dimension=0, tiled=True)
     masked = result * flat_flags.astype(jnp.float32)[:, None]

time: 580 us -> 564 us (0.972)
  waiting for transfers between devices: 245 us -> 214 us
  blocking collectives: 226 us -> 240 us
    all_gather x1 -> x0, waiting for transfers between devices: 31.1 us -> none  [body(): both_rows = lax.all_gather(flat_rows, 'dp', axis=0, tiled=True)]
    all_to_all x0 -> x1, blocking collectives: none -> 19.3 us  [body(): lax.all_to_all(jnp.stack([flat_rows] * lax.axis_size('dp')), 'dp', 0, 0)]
  transfers between devices with their start and end apart: 3 -> 2, of which waited for: 3 -> 2; matrix products, arithmetic and copies ran while one was open for 0% -> 0% of each run, Pallas kernels for 0% -> 0%
where the time goes in v1:
time: 564 us
  blocking collectives  240 us (43%)
  waiting for transfers between devices  214 us (38%)
  matrix products  49.4 us (9%)
  local copies, waits for them, and re-layouts  19.9 us (4%)
  starting transfers between devices  14.5 us (3%)
  between operations  13.5 us (2%)
  other arithmetic  12.9 us (2%)
    all_to_all x1, blocking collectives, body(): lax.all_to_all(outgoing, 'expert', split_axis=0, concat_axis=0, tiled=True)  201 us
    all_to_all x1, waiting for transfers between devices, body(): lax.all_to_all(answered, 'expert', split_axis=0, concat_axis=0, tiled=True)  187 us
    reduce_scatter x1, waiting for transfers between devices, body(): lax.psum_scatter(partial_out, 'dp', scatter_dimension=0, tiled=True)  27 us
    all_to_all x1, blocking collectives, body(): lax.all_to_all(jnp.stack([flat_rows] * lax.axis_size('dp')), 'dp', 0, 0)  19.3 us
    all_to_all x1, blocking collectives, body(): lax.all_to_all(present, 'expert', split_axis=0, concat_axis=0, tiled=True)  19 us
    dot_general x1, matrix products, swiglu(): gate_act = jnp.dot(row_block, w_gate, preferred_element_type=jnp.float32)  15.2 us
    dot_general x1, matrix products, swiglu(): return jnp.dot(hidden, w_down, preferred_element_type=jnp.float32)  14.5 us
    all_to_all x1, starting transfers between devices, body(): lax.all_to_all(answered, 'expert', split_axis=0, concat_axis=0, tiled=True)  14.5 us
  transfers between devices with their start and end apart: 2, of which 2 were waited for; matrix products, arithmetic and copies ran while one was open for 0% of the time, Pallas kernels for 0%

profile of v1, /device:TPU:2, one launch (start us, length us, event | category | flops | bytes accessed | tf_op | source)
XLA Modules:
  0.0 564.0 jit_solution(18133866929426200479)
XLA Ops:
  6.5 0.0 copy-start
  6.5 0.0 reduce-scatter.2.cloned.1.call-start
  6.5 0.8 bitcast_or_fusion
  7.4 0.9 copy.35
  8.3 0.1 copy.36
  8.4 0.1 reshape.50
  8.4 0.1 convert_reduce_fusion.1
  8.6 0.1 reduce_window_sum.11
  8.7 0.0 copy-start.3
  8.7 3.6 gather_fusion.1
  12.3 0.1 reshape.53
  12.4 0.1 copy.37
  12.5 0.0 copy-done.3
  12.5 0.1 copy.38
  12.6 0.7 convert_reduce_fusion
  13.3 3.4 convert_bitcast_fusion
  16.7 201.4 %all_to_all.25 = bf16[128,8,4096]{2,1,0:T(8,128)(2,1)S(1)} all-to-all(bf16[128,8,4096]{2,1,0:T(8,128)(2,1)S(1)} %convert_bitcast_fusion), channel_id=1, replica_groups=mesh['expert'=128,'dp'=2] {'expert'}, dimensions={0} | all-to-all | bytes 16777216 | tf_op jit(solution)/shard_map/all_to_all | solution.py:40
  218.1 1.5 pad_maximum_fusion
  219.7 0.0 copy-start.5
  219.7 19.3 %all_to_all.26 = bf16[2,1024,4096]{2,1,0:T(8,128)(2,1)} all-to-all(bf16[2,1024,4096]{2,1,0:T(8,128)(2,1)S(1)} %pad_maximum_fusion), channel_id=1, replica_groups=mesh['expert'=128,'dp'=2] {'dp'}, dimensions={0} | all-to-all | bytes 33554432 | tf_op jit(solution)/shard_map/all_to_all | solution.py:47
  239.0 0.0 copy-done.5
  239.0 0.0 copy-start.2
  239.0 0.0 copy-start.6
  239.0 15.2 %fusion.6 = f32[2048,384]{1,0:T(8,128)} fusion(bf16[2048,4096]{1,0:T(8,128)(2,1)} %bitcast.36, bf16[1,4096,384]{2,1,0:T(8,128)(2,1)S(1)} %copy-done.5), kind=kOutput, calls=%fused_computation.12 | convolution fusion | flops 6442450944 | bytes 23068672 | tf_op jit(solution)/shard_map/dot_general | solution.py:8
  254.3 0.0 copy-done.2
  254.3 0.0 copy-done.6
  254.3 10.6 %fusion.8 = bf16[2048,384]{1,0:T(8,128)(2,1)S(1)} fusion(bf16[2048,4096]{1,0:T(8,128)(2,1)S(1)} %bitcast.37, bf16[1,4096,384]{2,1,0:T(8,128)(2,1)S(1)} %copy-done.6, f32[2048,384]{1,0:T(8,128)} %fusion.6), kind=kOutput, calls=%fused_computation.14 | convolution fusion | flops 6447169536 | bytes 24641536 | tf_op jit(solution)/shard_map/dot_general | solution.py:9
  264.9 0.0 copy-done
  264.9 14.5 %fusion.3 = f32[2048,4096]{1,0:T(8,128)} fusion(bf16[2048,384]{1,0:T(8,128)(2,1)S(1)} %fusion.8, bf16[1,384,4096]{2,1,0:T(8,128)(2,1)S(1)} %copy-done), kind=kOutput, calls=%fused_computation.9 | convolution fusion | flops 6442450944 | bytes 38273024 | tf_op jit(solution)/shard_map/dot_general | solution.py:11
  279.3 0.0 reduce-scatter.2.cloned.1.call-update
  279.4 0.1 all_to_all.20
  279.5 19.0 %all_to_all.27 = bf16[128,1,8]{2,1,0:T(2,128)(2,1)S(1)} all-to-all(bf16[128,1,8]{2,1,0:T(2,128)(2,1)S(1)} %all_to_all.20), channel_id=1, replica_groups=mesh['expert'=128,'dp'=2] {'expert'}, dimensions={0} | all-to-all | bytes 4096 | tf_op jit(solution)/shard_map/all_to_all | solution.py:41
  298.5 0.2 convert_reduce_fusion.2
  298.7 0.1 reshape.41
  298.8 27.0 %reduce-scatter.2.cloned.1.call-done = f32[1024,4096]{1,0:T(8,128)} async-done(((f32[2048,4096]{1,0:T(8,128)}), f32[1024,4096]{1,0:T(8,128)}) %reduce-scatter.2.cloned.1.call-update) | async-done | bytes 16777232 | tf_op jit(solution)/shard_map/reduce_scatter | solution.py:50
  325.8 9.3 %fusion = bf16[128,8,4096]{2,1,0:T(8,128)(2,1)} fusion(f32[1024,4096]{1,0:T(8,128)} %reduce-scatter.2.cloned.1.call-done, f32[1024]{0:T(1024)S(1)} %reshape.41), kind=kLoop, calls=%fused_computation.4 | loop fusion | flops 8388608 | bytes 25169920 | tf_op jit(solution)/shard_map/reshape | solution.py:52
  335.1 0.0 copy-start.4
  335.1 14.5 %all-to-all-start.3 = ((bf16[128,8,4096]{2,1,0:T(8,128)(2,1)}), bf16[128,8,4096]{2,1,0:T(8,128)(2,1)}, u32[]{:S(2)}, u32[]{:S(2)}) async-start(bf16[128,8,4096]{2,1,0:T(8,128)(2,1)} %fusion), calls=%async_computation.4 | async-start | bytes 16777216 | tf_op jit(solution)/shard_map/all_to_all | solution.py:53
  349.6 0.0 copy-done.4
  349.6 0.1 copy.41
  349.7 0.1 copy.40
  349.8 0.1 reshape.44
  349.9 187.1 %all-to-all-done.3 = bf16[128,8,4096]{2,1,0:T(8,128)(2,1)} async-done(((bf16[128,8,4096]{2,1,0:T(8,128)(2,1)}), bf16[128,8,4096]{2,1,0:T(8,128)(2,1)}, u32[]{:S(2)}, u32[]{:S(2)}) %all-to-all-start.3) | async-done | bytes 8388640 | tf_op jit(solution)/shard_map/all_to_all | solution.py:53
  536.9 0.0 copy-start.1
  536.9 13.2 %gather_fusion = bf16[512,4096]{1,0:T(8,128)(2,1)} fusion(bf16[1024,4096]{1,0:T(8,128)(2,1)} %bitcast.8, s32[1024]{0:T(1024)S(1)} %pad_clamp_fusion), kind=kCustom, calls=%fused_computation | custom fusion | bytes 8390656 | tf_op jit(solution)/shard_map/gather | solution.py:54
  550.1 5.7 %fusion.1 = bf16[64,1,4096]{2,1,0:T(2,128)(2,1)S(1)} fusion(f32[64,8,1]{1,2,0:T(1,128)S(1)} %copy.41, bf16[512,4096]{1,0:T(8,128)(2,1)} %gather_fusion), kind=kOutput, calls=%fused_computation.6 | convolution fusion | flops 25165824 | bytes 4720640 | tf_op jit(solution)/shard_map/tk,tkd->td/dot_general | solution.py:55
  555.8 1.4 copy.44
  557.2 0.0 copy-done.1
  (4 shorter events, 0.1 us)
Async XLA Ops:
  6.5 258.3 %copy-start = (bf16[1,384,4096]{2,1,0:T(8,128)(2,1)S(1)}, bf16[1,384,4096]{2,1,0:T(8,128)(2,1)}, u32[]{:S(2)}) copy-start(bf16[1,384,4096]{2,1,0:T(8,128)(2,1)} %param.11) | copy-start | bytes 9437188
  6.5 319.3 %reduce-scatter.2.cloned.1.call-start = ((), (), s32[]{:S(2)}) async-start(), calls=%async_computation.5 | async-start | bytes 50331648 | tf_op jit(solution)/shard_map/reduce_scatter | solution.py:50
  8.7 3.8 copy-start.3
  219.7 19.3 %copy-start.5 = (bf16[1,4096,384]{2,1,0:T(8,128)(2,1)S(1)}, bf16[1,4096,384]{2,1,0:T(8,128)(2,1)}, u32[]{:S(2)}) copy-start(bf16[1,4096,384]{2,1,0:T(8,128)(2,1)} %param.9) | copy-start | bytes 9437188
  239.0 15.3 %copy-start.2 = (bf16[2,1024,4096]{2,1,0:T(8,128)(2,1)S(1)}, bf16[2,1024,4096]{2,1,0:T(8,128)(2,1)}, u32[]{:S(2)}) copy-start(bf16[2,1024,4096]{2,1,0:T(8,128)(2,1)} %all_to_all.26) | copy-start | bytes 50331652
  239.0 15.3 %copy-start.6 = (bf16[1,4096,384]{2,1,0:T(8,128)(2,1)S(1)}, bf16[1,4096,384]{2,1,0:T(8,128)(2,1)}, u32[]{:S(2)}) copy-start(bf16[1,4096,384]{2,1,0:T(8,128)(2,1)} %param.10) | copy-start | bytes 9437188
  335.1 14.5 %copy-start.4 = (f32[64,8]{0,1:T(8,128)S(1)}, f32[64,8]{0,1:T(8,128)}, u32[]{:S(2)}) copy-start(f32[64,8]{0,1:T(8,128)} %param.8) | copy-start | bytes 6148
  335.1 201.8 %all-to-all-start.3 = ((bf16[128,8,4096]{2,1,0:T(8,128)(2,1)}), bf16[128,8,4096]{2,1,0:T(8,128)(2,1)}, u32[]{:S(2)}, u32[]{:S(2)}) async-start(bf16[128,8,4096]{2,1,0:T(8,128)(2,1)} %fusion), calls=%async_computation.4 | async-start | bytes 16777216 | tf_op jit(solution)/shard_map/all_to_all | solution.py:53
  536.9 20.3 %copy-start.1 = (bf16[1,384,4096]{2,1,0:T(8,128)(2,1)S(1)}, bf16[1,384,4096]{2,1,0:T(8,128)(2,1)}, u32[]{:S(2)}) copy-start(bf16[1,384,4096]{2,1,0:T(8,128)(2,1)} %param.11) | copy-start | bytes 9437188
Sparse Core Ops, SparseCore 0:
  279.5 46.2 reduce-scatter.1
